TPU v7x, 512 devices: a whole 4x4x16 slice. The times are simulated.
512 devices in a mesh: grp: 16 (over y_lo, x, core), ep: 32 (over z, y_hi).
Axes of the slice: x: 4, y: 4 (y_hi: 2, y_lo: 2; y = y_hi * 2 + y_lo), z: 16, core: 2. Of those that a mesh axis runs over, the one named last changes fastest.
Arguments:
- tokens: bfloat16 [16, 512, 5120], P('grp', 'ep'), may hold values from -6 to 6
- cotangent: bfloat16 [16, 512, 5120], P('grp', 'ep'), may hold values from -1.5 to 1.5
- counts: int32 [16, 32, 4], P('grp', 'ep'), may hold values from 0 to 4, as said below
- destination: int32 [16, 32, 16], P('grp', 'ep'), may hold values from 0 to 15, each once within a row
- placement: int32 [32], replicated, may hold values from 0 to 31, each once
- gate_up_weight: bfloat16 [32, 2, 5120, 128], P('ep', None, 'grp'), may hold values from -0.078125 to 0.078125
- down_weight: bfloat16 [32, 5120, 128], P('ep', 'grp'), may hold values from -0.1875 to 0.1875
Outputs:
- layer_out: bfloat16 [16, 512, 5120], P('grp', 'ep')
- input_grad: bfloat16 [16, 512, 5120], P('grp', 'ep')
- gate_up_grad: float32 [32, 2, 5120, 128], P('ep', None, 'grp')
- down_grad: float32 [32, 5120, 128], P('ep', 'grp')
Inputs may be any that keep to these rules, and one draw needn't show every extreme that they name: counts[g, j, e] is the number of kept slots of expert e on device (g, j) after reassignment; some device has all 4 slots of an expert kept in every draw. `destination`: the 16 blocks of one device go to 16 different groups. `placement`: each expert slice is served by exactly one owner.
All inputs are finite; a program needn't handle non-finite values.
Results may differ from a plain program's by a relative error of at most 0.017.
Values may be sent and summed in bfloat16 or wider, within the bound.
No kernel may reach another device: no remote copies, remote signals or barrier semaphores. Data moves between devices by JAX's collectives and lax.ppermute only.
A program may use at most 64 MiB of HBM per device.

v0:
```python
import jax
import jax.numpy as jnp
from jax import lax
from jax.sharding import PartitionSpec as P


def swiglu_backward(gate_up, hidden_grad):
    gate_part = gate_up[0]
    up_part = gate_up[1]
    sigmoid_gate = jax.nn.sigmoid(gate_part)
    activated = gate_part * sigmoid_gate
    hidden = (activated * up_part).astype(jnp.bfloat16)
    gate_grad = hidden_grad * up_part * sigmoid_gate * (1.0 + gate_part * (1.0 - sigmoid_gate))
    up_grad = hidden_grad * activated
    return (hidden, jnp.stack([gate_grad, up_grad]).astype(jnp.bfloat16))


def body(tokens, cotangent, counts, destination, placement, gate_up_weight, down_weight):
    groups = lax.axis_size("grp")
    owners = lax.axis_size("ep")
    tok_dev = tokens.shape[1]
    model_width = tokens.shape[2]
    experts = counts.shape[2]
    capacity = tok_dev // experts
    block_rows = tok_dev // groups
    split_count = owners // experts
    row_count = owners * capacity
    order = jnp.argsort(destination[0, 0])
    send_tokens = jnp.take(tokens[0].reshape(groups, block_rows, model_width), order, axis=0)
    send_cotangent = jnp.take(cotangent[0].reshape(groups, block_rows, model_width), order, axis=0)
    here_tokens, here_cotangent = (
        lax.all_to_all(send_tokens, "grp", split_axis=0, concat_axis=0, tiled=True),
        lax.all_to_all(send_cotangent, "grp", split_axis=0, concat_axis=0, tiled=True),
    )
    slot_ids = lax.broadcasted_iota(jnp.int32, (experts, capacity), 1)
    keep = (slot_ids < counts[0, 0][:, None])[:, :, None]
    nothing = jnp.zeros((), jnp.bfloat16)
    kept_tokens = jnp.where(keep, here_tokens.reshape(experts, capacity, model_width), nothing)
    kept_cotangent = jnp.where(
        keep, here_cotangent.reshape(experts, capacity, model_width), nothing
    )
    expert_of = placement // split_count
    routed_tokens, routed_cotangent = (
        lax.all_to_all(
            jnp.take(kept_tokens, expert_of, axis=0), "ep", split_axis=0, concat_axis=0, tiled=True
        ),
        lax.all_to_all(
            jnp.take(kept_cotangent, expert_of, axis=0),
            "ep",
            split_axis=0,
            concat_axis=0,
            tiled=True,
        ),
    )
    routed_tokens = routed_tokens.reshape(row_count, model_width)
    routed_cotangent = routed_cotangent.reshape(row_count, model_width)
    stacked_down = down_weight[:, None]
    full_gate_up, full_down = (
        lax.all_gather(gate_up_weight, "grp", axis=2, tiled=True),
        lax.all_gather(stacked_down, "grp", axis=2, tiled=True),
    )
    full_gate_up = full_gate_up[0]
    full_down = full_down[0, 0]
    gate_up = jnp.einsum(
        "rd,kds->krs", routed_tokens, full_gate_up, preferred_element_type=jnp.float32
    )
    hidden_grad = jnp.dot(routed_cotangent, full_down, preferred_element_type=jnp.float32)
    hidden, grad_rows = swiglu_backward(gate_up, hidden_grad)
    forward_part = (
        jnp.einsum("rs,ds->rd", hidden, full_down, preferred_element_type=jnp.float32)
        .astype(jnp.bfloat16)
        .reshape(owners, capacity, model_width)
    )
    backward_part = (
        jnp.einsum("krs,kds->rd", grad_rows, full_gate_up, preferred_element_type=jnp.float32)
        .astype(jnp.bfloat16)
        .reshape(owners, capacity, model_width)
    )
    owner_table = (
        expert_of[:, None] == lax.broadcasted_iota(jnp.int32, (owners, experts), 1)
    ).astype(jnp.bfloat16)

    def combine(returned):
        summed = jnp.einsum(
            "jcd,je->ecd", returned, owner_table, preferred_element_type=jnp.float32
        )
        return summed.astype(jnp.bfloat16).reshape(1, tok_dev, model_width)

    layer_out = combine(lax.all_to_all(forward_part, "ep", split_axis=0, concat_axis=0, tiled=True))
    input_grad = combine(
        lax.all_to_all(backward_part, "ep", split_axis=0, concat_axis=0, tiled=True)
    )
    gate_up_term = jnp.einsum(
        "rd,krs->kds", routed_tokens, grad_rows, preferred_element_type=jnp.float32
    )
    down_term = jnp.einsum(
        "rd,rs->ds", routed_cotangent, hidden, preferred_element_type=jnp.float32
    )
    gate_up_grad, down_grad = (
        lax.psum_scatter(
            gate_up_term[None].astype(jnp.bfloat16), "grp", scatter_dimension=2, tiled=True
        ).astype(jnp.float32),
        lax.psum_scatter(
            down_term[None, None].astype(jnp.bfloat16), "grp", scatter_dimension=2, tiled=True
        ).astype(jnp.float32),
    )
    return (layer_out, input_grad, gate_up_grad, down_grad[:, 0])


def solution(mesh):
    return jax.shard_map(
        body,
        mesh=mesh,
        in_specs=(
            P("grp", "ep", None),
            P("grp", "ep", None),
            P("grp", "ep", None),
            P("grp", "ep", None),
            P(),
            P("ep", None, "grp", None),
            P("ep", "grp", None),
        ),
        out_specs=(
            P("grp", "ep", None),
            P("grp", "ep", None),
            P("ep", None, "grp", None),
            P("ep", "grp", None),
        ),
        check_vma=False,
    )
```

profile of v0, /device:TPU:32, one launch (start us, length us, event | category | flops | bytes accessed | tf_op | source)
XLA Modules:
  0.0 448.5 jit_solution(12998677638847090264)
XLA Ops:
  7.2 1.9 sort.17
  9.2 0.6 gather_fusion.2
  9.8 0.6 gather_fusion
  10.5 0.1 bitcast_select_fusion
  10.6 0.5 broadcast.114
  11.1 0.7 reduce.3
  11.8 0.8 reshape.164
  12.6 5.4 %all-to-all-start = ((bf16[16,2,2560]{2,1,0:T(2,128)(2,1)}), bf16[16,2,2560]{2,1,0:T(2,128)(2,1)S(1)}, u32[]{:S(2)}, u32[]{:S(2)}) async-start(bf16[16,2,2560]{2,1,0:T(2,128)(2,1)} %reshape.164), calls=%async_computation | async-start | bytes 327680 | tf_op jit(solution)/shard_map/all_to_all | solution.py:32
  18.1 0.7 reduce.2
  18.8 0.8 reshape.166
  19.6 0.1 iota_compare_fusion
  19.6 5.2 %all-to-all-done = bf16[16,2,2560]{2,1,0:T(2,128)(2,1)S(1)} async-done(((bf16[16,2,2560]{2,1,0:T(2,128)(2,1)}), bf16[16,2,2560]{2,1,0:T(2,128)(2,1)S(1)}, u32[]{:S(2)}, u32[]{:S(2)}) %all-to-all-start) | async-done | bytes 163872 | tf_op jit(solution)/shard_map/all_to_all | solution.py:32
  24.8 3.5 all-to-all-start.3
  28.3 0.1 reshape.165
  28.5 0.9 reduce
  29.4 0.1 reshape.94
  29.5 5.5 %all-to-all-done.3 = bf16[16,2,2560]{2,1,0:T(2,128)(2,1)S(1)} async-done(((bf16[16,2,2560]{2,1,0:T(2,128)(2,1)}), bf16[16,2,2560]{2,1,0:T(2,128)(2,1)S(1)}, u32[]{:S(2)}, u32[]{:S(2)}) %all-to-all-start.3) | async-done | bytes 163872 | tf_op jit(solution)/shard_map/all_to_all | solution.py:33
  35.0 0.1 reshape.167
  35.2 0.9 reduce.1
  36.1 0.1 reshape.98
  36.2 0.2 broadcast_select_fusion.2
  36.4 1.7 gather_fusion.3
  38.1 1.7 gather_fusion.1
  39.8 2.7 broadcast_select_fusion
  42.5 17.7 %all-to-all-start.1 = ((bf16[32,4,5120]{2,1,0:T(4,128)(2,1)}), bf16[32,4,5120]{2,1,0:T(4,128)(2,1)S(1)}, u32[]{:S(2)}, u32[]{:S(2)}) async-start(bf16[32,4,5120]{2,1,0:T(4,128)(2,1)} %get-tuple-element.29), calls=%async_computation.1 | async-start | bytes 2621440 | tf_op jit(solution)/shard_map/all_to_all | solution.py:44
  60.2 0.0 all-gather.4.cloned.1.call-start
  60.2 0.7 all-gather.4.cloned.1.call-update
  60.9 64.1 %all-to-all-done.1 = bf16[32,4,5120]{2,1,0:T(4,128)(2,1)S(1)} async-done(((bf16[32,4,5120]{2,1,0:T(4,128)(2,1)}), bf16[32,4,5120]{2,1,0:T(4,128)(2,1)S(1)}, u32[]{:S(2)}, u32[]{:S(2)}) %all-to-all-start.1) | async-done | bytes 1310752 | tf_op jit(solution)/shard_map/all_to_all | solution.py:44
  125.0 1.1 copy-done.3
  126.1 6.9 %all-to-all-start.4 = ((bf16[32,4,5120]{2,1,0:T(4,128)(2,1)}), bf16[32,4,5120]{2,1,0:T(4,128)(2,1)S(1)}, u32[]{:S(2)}, u32[]{:S(2)}) async-start(bf16[32,4,5120]{2,1,0:T(4,128)(2,1)} %get-tuple-element.28), calls=%async_computation.4 | async-start | bytes 2621440 | tf_op jit(solution)/shard_map/all_to_all | solution.py:47
  133.0 0.0 all-gather.6.cloned.1.call-start
  133.1 0.7 all-gather.6.cloned.1.call-update
  133.8 2.5 reshape.157
  136.3 0.0 all-gather.4.cloned.1.call-done
  136.3 2.3 fusion.11
  138.6 37.2 %all-gather.6.cloned.1.call-done = bf16[1,5120,128]{2,1,0:T(8,128)(2,1)} async-done(((bf16[1,320,128]{2,1,0:T(8,128)(2,1)}), bf16[1,5120,128]{2,1,0:T(8,128)(2,1)}) %all-gather.6.cloned.1.call-update) | async-done | bytes 1310736 | tf_op jit(solution)/shard_map/all_gather | solution.py:60
  175.8 2.9 convolution_convert_fusion.2
  178.7 3.4 reshape.96
  182.1 15.2 %all-to-all-done.4 = bf16[32,4,5120]{2,1,0:T(4,128)(2,1)S(1)} async-done(((bf16[32,4,5120]{2,1,0:T(4,128)(2,1)}), bf16[32,4,5120]{2,1,0:T(4,128)(2,1)S(1)}, u32[]{:S(2)}, u32[]{:S(2)}) %all-to-all-start.4) | async-done | bytes 1310752 | tf_op jit(solution)/shard_map/all_to_all | solution.py:47
  197.3 1.0 copy-done.2
  198.3 7.1 %all-to-all-start.2 = ((bf16[32,4,5120]{2,1,0:T(4,128)(2,1)}), bf16[32,4,5120]{2,1,0:T(4,128)(2,1)}, u32[]{:S(2)}, u32[]{:S(2)}) async-start(bf16[32,4,5120]{2,1,0:T(4,128)(2,1)} %reshape.96), calls=%async_computation.2 | async-start | bytes 2621440 | tf_op jit(solution)/shard_map/all_to_all | solution.py:89
  205.4 0.2 all-reduce.3.cloned.1.call-start
  205.6 2.5 reshape.99
  208.1 1.8 fusion.26
  209.9 2.3 fusion
  212.3 7.4 %copy.37 = bf16[1,2,5120,128]{3,1,0,2:T(2,128)(2,1)} copy(bf16[1,2,5120,128]{2,3,1,0:T(8,128)(2,1)} %fusion) | data formatting | bytes 5242880 | tf_op jit(solution)/shard_map/convert_element_type | solution.py:101
  219.7 2.7 fusion.1
  222.4 1.4 reshape.100
  223.8 46.0 %all-to-all-done.2 = bf16[32,4,5120]{2,1,0:T(4,128)(2,1)} async-done(((bf16[32,4,5120]{2,1,0:T(4,128)(2,1)}), bf16[32,4,5120]{2,1,0:T(4,128)(2,1)}, u32[]{:S(2)}, u32[]{:S(2)}) %all-to-all-start.2) | async-done | bytes 1310752 | tf_op jit(solution)/shard_map/all_to_all | solution.py:89
  269.8 7.0 %all-to-all-start.5 = ((bf16[32,4,5120]{2,1,0:T(4,128)(2,1)}), bf16[32,4,5120]{2,1,0:T(4,128)(2,1)S(1)}, u32[]{:S(2)}, u32[]{:S(2)}) async-start(bf16[32,4,5120]{2,1,0:T(4,128)(2,1)} %reshape.100), calls=%async_computation.5 | async-start | bytes 2621440 | tf_op jit(solution)/shard_map/all_to_all | solution.py:91
  276.8 0.0 reduce-scatter.2.cloned.1.call-start
  276.9 1.6 fusion.2
  278.5 1.3 dynamic-slice
  280.4 81.9 %all-reduce.3.cloned.1.call-done = bf16[1,2,5120,128]{3,1,0,2:T(2,128)(2,1)} async-done(((bf16[1,2,5120,128]{3,1,0,2:T(2,128)(2,1)}), bf16[1,2,5120,128]{3,1,0,2:T(2,128)(2,1)}) %all-reduce.3.cloned.1.call-update) | async-done | bytes 2621456
  362.3 1.0 dynamic-slice_convert_fusion
  363.4 0.7 copy.38
  364.1 71.7 %reduce-scatter.2.cloned.1.call-done = bf16[1,1,320,128]{3,2,1,0:T(8,128)(2,1)} async-done(((bf16[1,1,5120,128]{3,2,1,0:T(8,128)(2,1)}), bf16[1,1,320,128]{3,2,1,0:T(8,128)(2,1)}) %reduce-scatter.2.cloned.1.call-update) | async-done | bytes 81936 | tf_op jit(solution)/shard_map/reduce_scatter | solution.py:103
  435.8 1.6 bitcast_convert_fusion
  437.4 2.1 convolution_convert_fusion.4
  439.5 0.1 copy.32
  439.6 0.7 reshape.97
  440.3 0.8 convolution_convert_fusion.3
  441.1 0.1 copy.35
  441.2 0.7 reshape.101
  (21 shorter events, 0.1 us)
Async XLA Ops:
  7.2 2.0 copy-start
  7.2 2.7 copy-start.1
  9.8 8.2 %copy-start.4 = (s32[32]{0:T(128)S(1)}, s32[32]{0:T(128)}, u32[]{:S(2)}) copy-start(s32[32]{0:T(128)} %param.15) | copy-start | bytes 388
  10.5 9.1 %copy-start.5 = (s32[1,1,4]{2,1,0:T(1,128)S(1)}, s32[1,1,4]{2,1,0:T(1,128)}, u32[]{:S(2)}) copy-start(s32[1,1,4]{2,1,0:T(1,128)} %param.13) | copy-start | bytes 52
  12.6 12.2 %all-to-all-start = ((bf16[16,2,2560]{2,1,0:T(2,128)(2,1)}), bf16[16,2,2560]{2,1,0:T(2,128)(2,1)S(1)}, u32[]{:S(2)}, u32[]{:S(2)}) async-start(bf16[16,2,2560]{2,1,0:T(2,128)(2,1)} %reshape.164), calls=%async_computation | async-start | bytes 327680 | tf_op jit(solution)/shard_map/all_to_all | solution.py:32
  24.8 10.2 %all-to-all-start.3 = ((bf16[16,2,2560]{2,1,0:T(2,128)(2,1)}), bf16[16,2,2560]{2,1,0:T(2,128)(2,1)S(1)}, u32[]{:S(2)}, u32[]{:S(2)}) async-start(bf16[16,2,2560]{2,1,0:T(2,128)(2,1)} %reshape.166), calls=%async_computation.3 | async-start | bytes 327680 | tf_op jit(solution)/shard_map/all_to_all | solution.py:33
  42.5 82.5 %all-to-all-start.1 = ((bf16[32,4,5120]{2,1,0:T(4,128)(2,1)}), bf16[32,4,5120]{2,1,0:T(4,128)(2,1)S(1)}, u32[]{:S(2)}, u32[]{:S(2)}) async-start(bf16[32,4,5120]{2,1,0:T(4,128)(2,1)} %get-tuple-element.29), calls=%async_computation.1 | async-start | bytes 2621440 | tf_op jit(solution)/shard_map/all_to_all | solution.py:44
  60.2 76.1 %all-gather.4.cloned.1.call-start = ((), (), s32[]{:S(2)}) async-start(), calls=%async_computation.7 | async-start | bytes 2785280 | tf_op jit(solution)/shard_map/all_gather | solution.py:59
  125.0 1.1 copy-start.3
  126.1 71.2 %all-to-all-start.4 = ((bf16[32,4,5120]{2,1,0:T(4,128)(2,1)}), bf16[32,4,5120]{2,1,0:T(4,128)(2,1)S(1)}, u32[]{:S(2)}, u32[]{:S(2)}) async-start(bf16[32,4,5120]{2,1,0:T(4,128)(2,1)} %get-tuple-element.28), calls=%async_computation.4 | async-start | bytes 2621440 | tf_op jit(solution)/shard_map/all_to_all | solution.py:47
  133.0 42.7 %all-gather.6.cloned.1.call-start = ((), (), s32[]{:S(2)}) async-start(), calls=%async_computation.9 | async-start | bytes 1392640 | tf_op jit(solution)/shard_map/all_gather | solution.py:60
  197.3 1.0 copy-start.2
  198.3 71.5 %all-to-all-start.2 = ((bf16[32,4,5120]{2,1,0:T(4,128)(2,1)}), bf16[32,4,5120]{2,1,0:T(4,128)(2,1)}, u32[]{:S(2)}, u32[]{:S(2)}) async-start(bf16[32,4,5120]{2,1,0:T(4,128)(2,1)} %reshape.96), calls=%async_computation.2 | async-start | bytes 2621440 | tf_op jit(solution)/shard_map/all_to_all | solution.py:89
  205.4 156.9 %all-reduce.3.cloned.1.call-start = ((), (), s32[]{:S(2)}) async-start(), calls=%async_computation.10 | async-start | bytes 5242880
  269.8 170.5 %all-to-all-start.5 = ((bf16[32,4,5120]{2,1,0:T(4,128)(2,1)}), bf16[32,4,5120]{2,1,0:T(4,128)(2,1)S(1)}, u32[]{:S(2)}, u32[]{:S(2)}) async-start(bf16[32,4,5120]{2,1,0:T(4,128)(2,1)} %reshape.100), calls=%async_computation.5 | async-start | bytes 2621440 | tf_op jit(solution)/shard_map/all_to_all | solution.py:91
  276.8 159.0 %reduce-scatter.2.cloned.1.call-start = ((), (), s32[]{:S(2)}) async-start(), calls=%async_computation.8 | async-start | bytes 1392640 | tf_op jit(solution)/shard_map/reduce_scatter | solution.py:103
Sparse Core Ops, SparseCore 0:
  63.1 41.9 all-gather.3
  136.0 39.7 all-gather.5
  219.8 142.4 all-reduce.2
  365.0 70.7 reduce-scatter.1
where the time goes:
time: 450 us; the launch traced here: 448 us
  waiting for transfers between devices  328 us (73%)
  starting transfers between devices  48 us (11%)
  local copies, waits for them, and re-layouts  30 us (7%)
  matrix products  16.6 us (4%)
  between operations  14.7 us (3%)
  other arithmetic  11 us (2%)
    unnamed x5, waiting for transfers between devices  83.3 us
    reduce_scatter x1, waiting for transfers between devices, body(): lax.psum_scatter(down_term[None, None].astype(jnp.bfloat16), 'grp', scatt...  71.7 us
    all_to_all x1, waiting for transfers between devices, body(): lax.all_to_all(jnp.take(kept_tokens, expert_of, axis=0), 'ep', split_axis...  64.1 us
    all_to_all x1, waiting for transfers between devices, body(): lax.all_to_all(forward_part, 'ep', split_axis=0, concat_axis=0, tiled=True)  46 us
    all_gather x1, waiting for transfers between devices, body(): lax.all_gather(stacked_down, 'grp', axis=2, tiled=True)  37.2 us
    all_to_all x1, starting transfers between devices, body(): lax.all_to_all(jnp.take(kept_tokens, expert_of, axis=0), 'ep', split_axis...  17.7 us
    all_to_all x1, waiting for transfers between devices, body(): lax.all_to_all(jnp.take(kept_cotangent, expert_of, axis=0), 'ep', split_a...  15.2 us
  transfers between devices with their start and end apart: 10, of which 8 were waited for; matrix products, arithmetic and copies ran while one was open for 9% of the time, Pallas kernels for 0%

commit v1 on v0

--- a/solution.py
+++ b/solution.py
@@ -57,7 +57,9 @@
     stacked_down = down_weight[:, None]
     full_gate_up, full_down = (
         lax.all_gather(gate_up_weight, "grp", axis=2, tiled=True),
-        lax.all_gather(stacked_down, "grp", axis=2, tiled=True),
+        jnp.concatenate(
+            lax.all_to_all(jnp.stack([stacked_down] * lax.axis_size("grp")), "grp", 0, 0), axis=2
+        ),
     )
     full_gate_up = full_gate_up[0]
     full_down = full_down[0, 0]

time: 450 us -> 467 us (1.038)
  waiting for transfers between devices: 328 us -> 336 us
  local copies, waits for them, and re-layouts: 30 us -> 35.9 us
    all_to_all x1, waiting for transfers between devices: 15.2 us -> 54.5 us  [body(): lax.all_to_all(jnp.take(kept_cotangent, expert_of, axis=0), 'ep', split_a...]
    all_gather x1 -> x0, waiting for transfers between devices: 37.2 us -> none  [body(): lax.all_gather(stacked_down, 'grp', axis=2, tiled=True)]
    all_to_all x0 -> x1, waiting for transfers between devices: none -> 9.46 us  [body(): lax.all_to_all(jnp.stack([stacked_down] * lax.axis_size('grp')), 'grp', 0...]
    unnamed x5 -> x4, waiting for transfers between devices: 83.3 us -> 83.6 us
  transfers between devices with their start and end apart: 10 -> 10, of which waited for: 8 -> 8; matrix products, arithmetic and copies ran while one was open for 9% -> 11% of each run, Pallas kernels for 0% -> 0%
where the time goes in v1:
time: 467 us; the launch traced here: 465 us
  waiting for transfers between devices  336 us (72%)
  starting transfers between devices  51.9 us (11%)
  local copies, waits for them, and re-layouts  35.9 us (8%)
  matrix products  14.7 us (3%)
  between operations  14.7 us (3%)
  other arithmetic  12.4 us (3%)
    unnamed x4, waiting for transfers between devices  83.6 us
    reduce_scatter x1, waiting for transfers between devices, body(): lax.psum_scatter(down_term[None, None].astype(jnp.bfloat16), 'grp', scatt...  71.8 us
    all_to_all x1, waiting for transfers between devices, body(): lax.all_to_all(jnp.take(kept_tokens, expert_of, axis=0), 'ep', split_axis...  63.8 us
    all_to_all x1, waiting for transfers between devices, body(): lax.all_to_all(jnp.take(kept_cotangent, expert_of, axis=0), 'ep', split_a...  54.5 us
    all_to_all x1, waiting for transfers between devices, body(): lax.all_to_all(forward_part, 'ep', split_axis=0, concat_axis=0, tiled=True)  42 us
    all_to_all x1, starting transfers between devices, body(): lax.all_to_all(jnp.take(kept_tokens, expert_of, axis=0), 'ep', split_axis...  17.7 us
    all_to_all x1, waiting for transfers between devices, body(): lax.all_to_all(jnp.stack([stacked_down] * lax.axis_size('grp')), 'grp', 0...  9.46 us
  transfers between devices with their start and end apart: 10, of which 8 were waited for; matrix products, arithmetic and copies ran while one was open for 11% of the time, Pallas kernels for 0%

profile of v1, /device:TPU:32, one launch (start us, length us, event | category | flops | bytes accessed | tf_op | source)
XLA Modules:
  0.0 465.3 jit_solution(4263457984447374391)
XLA Ops:
  7.2 1.9 sort.17
  9.2 0.6 gather_fusion.2
  9.8 0.6 gather_fusion
  10.5 0.1 bitcast_select_fusion
  10.6 0.5 broadcast.117
  11.1 0.7 reduce.3
  11.8 0.8 reshape.165
  12.6 5.5 %all-to-all-start = ((bf16[16,2,2560]{2,1,0:T(2,128)(2,1)}), bf16[16,2,2560]{2,1,0:T(2,128)(2,1)S(1)}, u32[]{:S(2)}, u32[]{:S(2)}) async-start(bf16[16,2,2560]{2,1,0:T(2,128)(2,1)} %reshape.165), calls=%async_computation | async-start | bytes 327680 | tf_op jit(solution)/shard_map/all_to_all | solution.py:32
  18.2 0.7 reduce.2
  18.9 0.8 reshape.167
  19.7 0.1 iota_compare_fusion
  19.8 5.2 %all-to-all-done = bf16[16,2,2560]{2,1,0:T(2,128)(2,1)S(1)} async-done(((bf16[16,2,2560]{2,1,0:T(2,128)(2,1)}), bf16[16,2,2560]{2,1,0:T(2,128)(2,1)S(1)}, u32[]{:S(2)}, u32[]{:S(2)}) %all-to-all-start) | async-done | bytes 163872 | tf_op jit(solution)/shard_map/all_to_all | solution.py:32
  24.9 3.5 all-to-all-start.4
  28.5 0.1 reshape.166
  28.6 0.9 reduce
  29.5 0.1 reshape.97
  29.6 5.5 %all-to-all-done.4 = bf16[16,2,2560]{2,1,0:T(2,128)(2,1)S(1)} async-done(((bf16[16,2,2560]{2,1,0:T(2,128)(2,1)}), bf16[16,2,2560]{2,1,0:T(2,128)(2,1)S(1)}, u32[]{:S(2)}, u32[]{:S(2)}) %all-to-all-start.4) | async-done | bytes 163872 | tf_op jit(solution)/shard_map/all_to_all | solution.py:33
  35.2 1.3 stack.15
  36.5 3.7 all-to-all-start.2
  40.2 0.1 reshape.168
  40.4 0.9 reduce.1
  41.3 0.1 reshape.101
  41.4 0.2 broadcast_select_fusion.2
  41.6 1.7 gather_fusion.3
  43.3 2.6 gather_fusion.1
  45.9 4.1 broadcast_select_fusion
  50.0 9.5 %all-to-all-done.2 = bf16[16,1,1,320,128]{4,3,2,1,0:T(8,128)(2,1)S(1)} async-done(((bf16[16,1,1,320,128]{4,3,2,1,0:T(8,128)(2,1)}), bf16[16,1,1,320,128]{4,3,2,1,0:T(8,128)(2,1)S(1)}, u32[]{:S(2)}, u32[]{:S(2)}) %all-to-all-start.2) | async-done | bytes 1310752 | tf_op jit(solution)/shard_map/all_to_all | solution.py:61
  59.4 17.7 %all-to-all-start.1 = ((bf16[32,4,5120]{2,1,0:T(4,128)(2,1)}), bf16[32,4,5120]{2,1,0:T(4,128)(2,1)S(1)}, u32[]{:S(2)}, u32[]{:S(2)}) async-start(bf16[32,4,5120]{2,1,0:T(4,128)(2,1)} %get-tuple-element.29), calls=%async_computation.1 | async-start | bytes 2621440 | tf_op jit(solution)/shard_map/all_to_all | solution.py:44
  77.1 0.0 all-gather.2.cloned.1.call-start
  77.2 0.7 all-gather.2.cloned.1.call-update
  77.9 63.8 %all-to-all-done.1 = bf16[32,4,5120]{2,1,0:T(4,128)(2,1)S(1)} async-done(((bf16[32,4,5120]{2,1,0:T(4,128)(2,1)}), bf16[32,4,5120]{2,1,0:T(4,128)(2,1)S(1)}, u32[]{:S(2)}, u32[]{:S(2)}) %all-to-all-start.1) | async-done | bytes 1310752 | tf_op jit(solution)/shard_map/all_to_all | solution.py:44
  141.7 1.1 copy-done.4
  142.8 7.0 %all-to-all-start.5 = ((bf16[32,4,5120]{2,1,0:T(4,128)(2,1)}), bf16[32,4,5120]{2,1,0:T(4,128)(2,1)}, u32[]{:S(2)}, u32[]{:S(2)}) async-start(bf16[32,4,5120]{2,1,0:T(4,128)(2,1)} %get-tuple-element.28), calls=%async_computation.5 | async-start | bytes 2621440 | tf_op jit(solution)/shard_map/all_to_all | solution.py:47
  149.8 2.5 reshape.158
  152.3 0.0 all-gather.2.cloned.1.call-done
  152.3 2.3 fusion.8
  154.6 1.6 convolution_convert_fusion.2
  156.2 3.4 reshape.99
  159.6 54.5 %all-to-all-done.5 = bf16[32,4,5120]{2,1,0:T(4,128)(2,1)} async-done(((bf16[32,4,5120]{2,1,0:T(4,128)(2,1)}), bf16[32,4,5120]{2,1,0:T(4,128)(2,1)}, u32[]{:S(2)}, u32[]{:S(2)}) %all-to-all-start.5) | async-done | bytes 1310752 | tf_op jit(solution)/shard_map/all_to_all | solution.py:47
  214.1 7.1 %all-to-all-start.3 = ((bf16[32,4,5120]{2,1,0:T(4,128)(2,1)}), bf16[32,4,5120]{2,1,0:T(4,128)(2,1)}, u32[]{:S(2)}, u32[]{:S(2)}) async-start(bf16[32,4,5120]{2,1,0:T(4,128)(2,1)} %reshape.99), calls=%async_computation.3 | async-start | bytes 2621440 | tf_op jit(solution)/shard_map/all_to_all | solution.py:91
  221.2 0.2 all-reduce.3.cloned.1.call-start
  221.4 3.3 reshape.102
  224.7 1.8 fusion.23
  226.5 2.4 fusion
  228.9 7.4 %copy.37 = bf16[1,2,5120,128]{3,1,0,2:T(2,128)(2,1)} copy(bf16[1,2,5120,128]{2,3,1,0:T(8,128)(2,1)} %fusion) | data formatting | bytes 5242880 | tf_op jit(solution)/shard_map/convert_element_type | solution.py:103
  236.3 1.7 copy-done.3
  238.1 2.0 fusion.1
  240.1 3.4 reshape.103
  243.5 42.0 %all-to-all-done.3 = bf16[32,4,5120]{2,1,0:T(4,128)(2,1)} async-done(((bf16[32,4,5120]{2,1,0:T(4,128)(2,1)}), bf16[32,4,5120]{2,1,0:T(4,128)(2,1)}, u32[]{:S(2)}, u32[]{:S(2)}) %all-to-all-start.3) | async-done | bytes 1310752 | tf_op jit(solution)/shard_map/all_to_all | solution.py:91
  285.6 7.0 %all-to-all-start.6 = ((bf16[32,4,5120]{2,1,0:T(4,128)(2,1)}), bf16[32,4,5120]{2,1,0:T(4,128)(2,1)S(1)}, u32[]{:S(2)}, u32[]{:S(2)}) async-start(bf16[32,4,5120]{2,1,0:T(4,128)(2,1)} %reshape.103), calls=%async_computation.6 | async-start | bytes 2621440 | tf_op jit(solution)/shard_map/all_to_all | solution.py:93
  292.6 0.0 reduce-scatter.2.cloned.1.call-start
  292.7 1.6 fusion.2
  294.3 1.3 dynamic-slice
  296.3 82.9 %all-reduce.3.cloned.1.call-done = bf16[1,2,5120,128]{3,1,0,2:T(2,128)(2,1)} async-done(((bf16[1,2,5120,128]{3,1,0,2:T(2,128)(2,1)}), bf16[1,2,5120,128]{3,1,0,2:T(2,128)(2,1)}) %all-reduce.3.cloned.1.call-update) | async-done | bytes 2621456
  379.1 1.0 dynamic-slice_convert_fusion
  380.1 0.7 copy.38
  380.9 71.8 %reduce-scatter.2.cloned.1.call-done = bf16[1,1,320,128]{3,2,1,0:T(8,128)(2,1)} async-done(((bf16[1,1,5120,128]{3,2,1,0:T(8,128)(2,1)}), bf16[1,1,320,128]{3,2,1,0:T(8,128)(2,1)}) %reduce-scatter.2.cloned.1.call-update) | async-done | bytes 81936 | tf_op jit(solution)/shard_map/reduce_scatter | solution.py:105
  452.6 1.6 bitcast_convert_fusion
  454.2 2.1 convolution_convert_fusion.4
  456.3 0.1 copy.32
  456.4 0.7 reshape.100
  457.1 0.8 convolution_convert_fusion.3
  458.0 0.1 copy.35
  458.1 0.7 reshape.104
  (25 shorter events, 0.1 us)
Async XLA Ops:
  7.2 2.0 copy-start
  7.2 2.7 copy-start.2
  9.8 8.3 %copy-start.6 = (s32[32]{0:T(128)S(1)}, s32[32]{0:T(128)}, u32[]{:S(2)}) copy-start(s32[32]{0:T(128)} %param.15) | copy-start | bytes 388
  10.5 9.2 %copy-start.7 = (s32[1,1,4]{2,1,0:T(1,128)S(1)}, s32[1,1,4]{2,1,0:T(1,128)}, u32[]{:S(2)}) copy-start(s32[1,1,4]{2,1,0:T(1,128)} %param.13) | copy-start | bytes 52
  12.6 22.5 %copy-start.5 = (bf16[1,320,128]{2,1,0:T(8,128)(2,1)S(1)}, bf16[1,320,128]{2,1,0:T(8,128)(2,1)}, u32[]{:S(2)}) copy-start(bf16[1,320,128]{2,1,0:T(8,128)(2,1)} %param.17) | copy-start | bytes 245764
  12.6 12.3 %all-to-all-start = ((bf16[16,2,2560]{2,1,0:T(2,128)(2,1)}), bf16[16,2,2560]{2,1,0:T(2,128)(2,1)S(1)}, u32[]{:S(2)}, u32[]{:S(2)}) async-start(bf16[16,2,2560]{2,1,0:T(2,128)(2,1)} %reshape.165), calls=%async_computation | async-start | bytes 327680 | tf_op jit(solution)/shard_map/all_to_all | solution.py:32
  24.9 10.2 %all-to-all-start.4 = ((bf16[16,2,2560]{2,1,0:T(2,128)(2,1)}), bf16[16,2,2560]{2,1,0:T(2,128)(2,1)S(1)}, u32[]{:S(2)}, u32[]{:S(2)}) async-start(bf16[16,2,2560]{2,1,0:T(2,128)(2,1)} %reshape.167), calls=%async_computation.4 | async-start | bytes 327680 | tf_op jit(solution)/shard_map/all_to_all | solution.py:33
  36.5 22.9 %all-to-all-start.2 = ((bf16[16,1,1,320,128]{4,3,2,1,0:T(8,128)(2,1)}), bf16[16,1,1,320,128]{4,3,2,1,0:T(8,128)(2,1)S(1)}, u32[]{:S(2)}, u32[]{:S(2)}) async-start(bf16[16,1,1,320,128]{4,3,2,1,0:T(8,128)(2,1)} %stack.15), calls=%async_computation.2 | async-start | bytes 2621440 | tf_op jit(solution)/shard_map/all_to_all | solution.py:61
  59.4 82.2 %all-to-all-start.1 = ((bf16[32,4,5120]{2,1,0:T(4,128)(2,1)}), bf16[32,4,5120]{2,1,0:T(4,128)(2,1)S(1)}, u32[]{:S(2)}, u32[]{:S(2)}) async-start(bf16[32,4,5120]{2,1,0:T(4,128)(2,1)} %get-tuple-element.29), calls=%async_computation.1 | async-start | bytes 2621440 | tf_op jit(solution)/shard_map/all_to_all | solution.py:44
  77.1 75.2 %all-gather.2.cloned.1.call-start = ((), (), s32[]{:S(2)}) async-start(), calls=%async_computation.8 | async-start | bytes 2785280 | tf_op jit(solution)/shard_map/all_gather | solution.py:59
  141.7 1.1 copy-start.4
  142.8 71.4 %all-to-all-start.5 = ((bf16[32,4,5120]{2,1,0:T(4,128)(2,1)}), bf16[32,4,5120]{2,1,0:T(4,128)(2,1)}, u32[]{:S(2)}, u32[]{:S(2)}) async-start(bf16[32,4,5120]{2,1,0:T(4,128)(2,1)} %get-tuple-element.28), calls=%async_computation.5 | async-start | bytes 2621440 | tf_op jit(solution)/shard_map/all_to_all | solution.py:47
  214.1 71.5 %all-to-all-start.3 = ((bf16[32,4,5120]{2,1,0:T(4,128)(2,1)}), bf16[32,4,5120]{2,1,0:T(4,128)(2,1)}, u32[]{:S(2)}, u32[]{:S(2)}) async-start(bf16[32,4,5120]{2,1,0:T(4,128)(2,1)} %reshape.99), calls=%async_computation.3 | async-start | bytes 2621440 | tf_op jit(solution)/shard_map/all_to_all | solution.py:91
  221.2 157.9 %all-reduce.3.cloned.1.call-start = ((), (), s32[]{:S(2)}) async-start(), calls=%async_computation.10 | async-start | bytes 5242880
  236.3 1.7 copy-start.3
  243.5 49.1 %copy-start.1 = (bf16[128,5120]{1,0:T(8,128)(2,1)S(1)}, bf16[128,5120]{1,0:T(8,128)(2,1)}, u32[]{:S(2)}) copy-start(bf16[128,5120]{1,0:T(8,128)(2,1)} %reshape.102) | copy-start | bytes 3932164
  285.6 171.6 %all-to-all-start.6 = ((bf16[32,4,5120]{2,1,0:T(4,128)(2,1)}), bf16[32,4,5120]{2,1,0:T(4,128)(2,1)S(1)}, u32[]{:S(2)}, u32[]{:S(2)}) async-start(bf16[32,4,5120]{2,1,0:T(4,128)(2,1)} %reshape.103), calls=%async_computation.6 | async-start | bytes 2621440 | tf_op jit(solution)/shard_map/all_to_all | solution.py:93
  292.6 160.0 %reduce-scatter.2.cloned.1.call-start = ((), (), s32[]{:S(2)}) async-start(), calls=%async_computation.9 | async-start | bytes 1392640 | tf_op jit(solution)/shard_map/reduce_scatter | solution.py:105
Sparse Core Ops, SparseCore 0:
  80.1 41.4 all-gather.1
  236.5 142.5 all-reduce.2
  381.9 70.6 reduce-scatter.1
